TPU v7x, 512 devices: a whole 4x4x16 slice. The times are simulated.
512 devices in a mesh: dp: 4 (over x), cand: 32 (over z, core), tensor: 4 (over y).
Axes of the slice: x: 4, y: 4, z: 16, core: 2. Of those that a mesh axis runs over, the one named last changes fastest.
Arguments:
- context: bfloat16 [8, 4096, 3584], P('dp', 'cand', 'tensor'), may hold values from -12 to 12
- residual: bfloat16 [8, 4096, 3584], P('dp', ('cand', 'tensor')), may hold values from -36 to 36
- out_weight: bfloat16 [3584, 3584], P('cand', 'tensor'), may hold values from -0.09375 to 0.09375
- adapter_down: bfloat16 [3584, 16], P('tensor'), may hold values from -0.09375 to 0.09375
- adapter_up_weight: bfloat16 [16, 3584], replicated, may hold values from -1.5 to 1.5
- norm_gain: float32 [3584], replicated, may hold values from 0.5 to 1.5
- score_weight: float32 [3584], replicated, may hold values from -0.09375 to 0.09375
- teacher: bfloat16 [8, 4096, 4096], P('dp', 'cand', 'tensor'), may hold values from 0.019897461 to 0.9765625
- pair_mask: int32 [8, 4096, 4096], P('dp', 'cand', 'tensor'), may hold values from 0 to 1, as said below
- loss_scale: float32 [8], P('dp'), may hold values from 65536 to 262144
Outputs:
- context_grad: bfloat16 [8, 4096, 3584], P('dp', 'cand', 'tensor')
- residual_gradient: bfloat16 [8, 4096, 3584], P('dp', ('cand', 'tensor'))
- down_grad: float32 [3584, 16], P('tensor')
- up_weight_gradient: float32 [16, 3584], P(None, 'tensor')
- pair_loss: float32 [8], P('dp')
Inputs may be any that keep to these rules, and one draw needn't show every extreme that they name: pair_mask holds 0 or 1; with P = 32, every pair (i, j) whose group j // P lies 4096 / (2P) groups after i // P, counted round over the 4096 / P groups, is valid.
All inputs are finite; a program needn't handle non-finite values.
Results may differ from a plain program's by a relative error of at most 0.02.
Values may be sent and summed in bfloat16 or wider, within the bound.
No kernel may reach another device: no remote copies, remote signals or barrier semaphores. Data moves between devices by JAX's collectives and lax.ppermute only.
A program may use at most 64 MiB of HBM per device.

v0:
```python
import jax
import jax.numpy as jnp
from jax import lax
from jax.sharding import PartitionSpec as P

ADAPTER_SCALE = 0.5
epsilon = 1e-06


def rounded(term):
    return lax.optimization_barrier(term.astype(jnp.bfloat16)).astype(jnp.float32)


def pair_terms(all_scores, own_scores, teacher, valid_pairs, row_start, col_start):
    column_scores = lax.dynamic_slice_in_dim(all_scores, col_start, teacher.shape[2], 1)
    margin = own_scores[:, :, None] - column_scores[:, None, :]
    target = teacher.astype(jnp.float32)
    total = jnp.sum(valid_pairs * (jax.nn.softplus(margin) - target * margin), axis=(1, 2))
    slope = valid_pairs * (jax.nn.sigmoid(margin) - target)
    blank = jnp.zeros(all_scores.shape, jnp.float32)
    row_part = lax.dynamic_update_slice_in_dim(blank, jnp.sum(slope, axis=2), row_start, 1)
    column_part = lax.dynamic_update_slice_in_dim(blank, jnp.sum(slope, axis=1), col_start, 1)
    return (total, row_part - column_part)


def on_device(
    context,
    residual,
    out_weight,
    adapter_down,
    adapter_up_weight,
    norm_gain,
    score_weight,
    teacher,
    pair_mask,
    loss_scale,
):
    cand_rows = context.shape[1]
    tensor_count = lax.axis_size("tensor")
    share = cand_rows // tensor_count
    tensor_index = lax.axis_index("tensor")
    group_index = lax.axis_index("cand")
    valid_pairs = pair_mask.astype(jnp.float32)
    mask_count = jnp.sum(valid_pairs, axis=(1, 2))
    count = lax.psum(mask_count, ("cand", "tensor"))
    low_terms = rounded(
        jnp.einsum("qch,hr->qcr", context, adapter_down, preferred_element_type=jnp.float32)
    )
    full_weight = lax.all_gather(out_weight, "cand", axis=0, tiled=True)
    head_terms = jnp.einsum("qch,dh->qcd", context, full_weight, preferred_element_type=jnp.float32)
    head_terms = rounded(head_terms)
    summed_output, low_sum = (
        lax.psum_scatter(
            head_terms.astype(jnp.bfloat16), "tensor", scatter_dimension=1, tiled=True
        ).astype(jnp.float32),
        lax.psum_scatter(
            low_terms.astype(jnp.bfloat16), "tensor", scatter_dimension=1, tiled=True
        ).astype(jnp.float32),
    )
    adapter_input_rows = low_sum.astype(jnp.bfloat16)
    lifted_rows = jnp.einsum(
        "qcr,rd->qcd", adapter_input_rows, adapter_up_weight, preferred_element_type=jnp.float32
    )
    hidden_state = (
        residual.astype(jnp.float32) + summed_output + ADAPTER_SCALE * lifted_rows
    ).astype(jnp.bfloat16)
    hidden_wide = hidden_state.astype(jnp.float32)
    inv_rms = lax.rsqrt(jnp.mean(hidden_wide * hidden_wide, axis=2, keepdims=True) + epsilon)
    scores = jnp.sum(hidden_wide * inv_rms * norm_gain * score_weight, axis=2)
    all_scores = lax.all_gather(scores, ("cand", "tensor"), axis=1, tiled=True)
    own_start = group_index * cand_rows + tensor_index * share
    row_start = group_index * cand_rows
    col_start = tensor_index * teacher.shape[2]
    own_scores = lax.dynamic_slice_in_dim(all_scores, row_start, cand_rows, 1)
    total, score_vector = pair_terms(
        all_scores, own_scores, teacher, valid_pairs, row_start, col_start
    )
    summed_grad, loss_sum = lax.psum((score_vector, total), ("cand", "tensor"))
    pair_loss = loss_sum / count
    factor = loss_scale / count
    score_grad = lax.dynamic_slice_in_dim(summed_grad, own_start, share, 1) * factor[:, None]
    back_step = score_grad[:, :, None] * norm_gain * score_weight
    grad_hidden = inv_rms * back_step - hidden_wide * inv_rms**3 * jnp.mean(
        hidden_wide * back_step, axis=2, keepdims=True
    )
    grad_rows = grad_hidden.astype(jnp.bfloat16)
    adapter_rows = (
        ADAPTER_SCALE
        * jnp.einsum(
            "qcd,rd->qcr", grad_rows, adapter_up_weight, preferred_element_type=jnp.float32
        )
    ).astype(jnp.bfloat16)
    full_grads, full_adapter = (
        lax.all_gather(grad_rows, "tensor", axis=1, tiled=True),
        lax.all_gather(adapter_rows, "tensor", axis=1, tiled=True),
    )
    up_partial_gradient = ADAPTER_SCALE * jnp.einsum(
        "qcr,qcd->rd", adapter_input_rows, grad_rows, preferred_element_type=jnp.float32
    )
    up_share = lax.psum_scatter(
        up_partial_gradient.astype(jnp.bfloat16), "tensor", scatter_dimension=1, tiled=True
    ).astype(jnp.float32)
    adapter_back = jnp.einsum(
        "qcr,hr->qch", full_adapter, adapter_down, preferred_element_type=jnp.float32
    )
    context_wide = (
        jnp.einsum("qcd,dh->qch", full_grads, full_weight, preferred_element_type=jnp.float32)
        + adapter_back
    )
    context_grad = context_wide.astype(jnp.bfloat16)
    down_local = jnp.einsum(
        "qch,qcr->hr", context, full_adapter, preferred_element_type=jnp.float32
    )
    down_grad, up_weight_gradient = lax.psum((down_local, up_share), ("dp", "cand"))
    return (context_grad, grad_rows, down_grad, up_weight_gradient, pair_loss)


def solution(mesh):
    in_specs = (
        P("dp", "cand", "tensor"),
        P("dp", ("cand", "tensor"), None),
        P("cand", "tensor"),
        P("tensor", None),
        P(),
        P(),
        P(),
        P("dp", "cand", "tensor"),
        P("dp", "cand", "tensor"),
        P("dp"),
    )
    out_specs = (
        P("dp", "cand", "tensor"),
        P("dp", ("cand", "tensor"), None),
        P("tensor", None),
        P(None, "tensor"),
        P("dp"),
    )
    return jax.shard_map(
        on_device, mesh=mesh, in_specs=in_specs, out_specs=out_specs, check_vma=False
    )
```

profile of v0, /device:TPU:16, one launch (start us, length us, event | category | flops | bytes accessed | tf_op | source)
XLA Modules:
  0.0 1309.3 jit_solution(4041656282521602248)
XLA Ops:
  8.1 0.7 all-gather.4.cloned.1.call-update
  8.8 0.2 copy-done
  9.0 0.9 convolution_convert_fusion
  10.0 0.2 copy.20
  10.2 0.7 reshape.41
  11.0 81.7 %all-gather.4.cloned.1.call-done = bf16[3584,896]{1,0:T(8,128)(2,1)} async-done(((bf16[112,896]{1,0:T(8,128)(2,1)}), bf16[3584,896]{1,0:T(8,128)(2,1)}) %all-gather.4.cloned.1.call-update) | async-done | bytes 6422544 | tf_op jit(solution)/shard_map/all_gather | solution.py:49
  92.7 6.2 fusion.4
  99.0 0.8 reshape.42
  99.8 0.7 copy.21
  100.4 29.0 %reduce-scatter.8.cloned.1.call-done = bf16[2,32,3584]{2,1,0:T(8,128)(2,1)} async-done(((bf16[2,128,3584]{2,1,0:T(8,128)(2,1)}), bf16[2,32,3584]{2,1,0:T(8,128)(2,1)}) %reduce-scatter.8.cloned.1.call-update) | async-done | bytes 458768 | tf_op jit(solution)/shard_map/reduce_scatter | solution.py:53
  129.5 1.5 multiply_reduce_fusion.2
  131.0 0.3 multiply_reduce_fusion.1
  131.3 140.3 %all-gather = f32[128,32,2]{1,2,0:T(2,128)S(1)} all-gather(f32[1,32,2]{1,2,0:T(2,128)S(1)} %bitcast.57), channel_id=1, replica_groups=mesh['dp'=4,'cand'=32,'tensor'=4] {'cand','tensor'}, dimensions={0}, use_global_device_ids=true | all-gather | bytes 33024 | tf_op jit(solution)/shard_map/all_gather | solution.py:70
  271.6 0.1 reshape.35
  271.8 1.2 fusion.24
  273.0 0.2 fusion.31
  273.3 493.2 %all-reduce = (f32[2,4096]{1,0:T(2,128)S(1)}, f32[2]{0:T(128)S(1)}, f32[2]{0:T(128)S(1)}) all-reduce(f32[2,4096]{1,0:T(2,128)S(1)} %sub.29, f32[2]{0:T(128)S(1)} %get-tuple-element.6, f32[2]{0:T(128)S(1)} %get-tuple-element.5), channel_id=1, replica_groups=mesh['dp'=4,'cand'=32,'tensor'=4] {'cand','tensor'}, use_global_device_ids=true, to_apply=%region_6.7 | all-reduce | flops 8196 | bytes 65568 | tf_op jit(solution)/shard_map/psum | solution.py:78
  766.4 1.2 fusion.32
  767.7 0.3 multiply_reduce_fusion
  768.0 0.3 subtract_convert_fusion
  768.3 0.2 fusion.11
  768.5 1.3 copy.22
  769.9 0.7 all-gather.6.cloned.1.call-update
  770.6 1.4 fusion.13
  772.0 0.1 copy.17
  772.1 13.7 %all_gather.15 = bf16[2,128,16]{2,0,1:T(2,128)(2,1)S(1)} all-gather(bf16[2,32,16]{2,0,1:T(2,128)(2,1)S(1)} %copy.17), channel_id=1, replica_groups=mesh['dp'=4,'cand'=32,'tensor'=4] {'tensor'}, dimensions={1}, use_global_device_ids=true | all-gather | bytes 10240 | tf_op jit(solution)/shard_map/all_gather | solution.py:95
  785.9 0.2 convolution_bitcast_fusion.1
  786.1 13.0 reduce-scatter.12.cloned.1.call-done
  799.1 1.0 copy.23
  800.1 495.1 %all-reduce.3 = (f32[896,16]{0,1:T(8,128)}, f32[16,896]{1,0:T(8,128)}) all-reduce(f32[896,16]{0,1:T(8,128)S(1)} %convolution_bitcast_fusion.1, bf16[16,896]{1,0:T(8,128)(2,1)S(1)} %copy.23), channel_id=1, replica_groups=mesh['dp'=4,'cand'=32,'tensor'=4] {'dp','cand'}, use_global_device_ids=true, to_apply=%region_10.11 | all-reduce | flops 28672 | bytes 200704 | tf_op jit(solution)/shard_map/psum | solution.py:114
  1295.2 5.5 fusion
  1300.6 1.1 fusion.12
  (41 shorter events, 0.6 us)
Async XLA Ops:
  8.0 1.0 copy-start
  8.0 84.7 %all-gather.4.cloned.1.call-start = ((), (), s32[]{:S(2)}) async-start(), calls=%async_computation.3 | async-start | bytes 6623232 | tf_op jit(solution)/shard_map/all_gather | solution.py:49
  8.7 90.2 %reduce-scatter.10.cloned.1.call-start = ((), (), s32[]{:S(2)}) async-start(), calls=%async_computation.6 | async-start | bytes 40960
  10.9 118.6 %copy-start.4 = (bf16[2,32,3584]{2,1,0:T(8,128)(2,1)S(1)}, bf16[2,32,3584]{2,1,0:T(8,128)(2,1)}, u32[]{:S(2)}) copy-start(bf16[2,32,3584]{2,1,0:T(8,128)(2,1)} %param.11) | copy-start | bytes 1376260
  10.9 118.6 %copy-start.5 = (bf16[16,3584]{1,0:T(8,128)(2,1)S(1)}, bf16[16,3584]{1,0:T(8,128)(2,1)}, u32[]{:S(2)}) copy-start(bf16[16,3584]{1,0:T(8,128)(2,1)} %param.14) | copy-start | bytes 344068
  10.9 120.1 %copy-start.6 = (f32[3584]{0:T(1024)S(1)}, f32[3584]{0:T(1024)}, u32[]{:S(2)}) copy-start(f32[3584]{0:T(1024)} %param.16) | copy-start | bytes 43012
  10.9 120.1 %copy-start.7 = (f32[3584]{0:T(1024)S(1)}, f32[3584]{0:T(1024)}, u32[]{:S(2)}) copy-start(f32[3584]{0:T(1024)} %param.15) | copy-start | bytes 43012
  10.9 260.8 %copy-start.2 = (s32[2,128,1024]{2,1,0:T(8,128)S(1)}, s32[2,128,1024]{2,1,0:T(8,128)}, u32[]{:S(2)}) copy-start(s32[2,128,1024]{2,1,0:T(8,128)} %param.18) | copy-start | bytes 3145732
  11.0 260.8 %copy-start.3 = (bf16[2,128,1024]{2,1,0:T(8,128)(2,1)S(1)}, bf16[2,128,1024]{2,1,0:T(8,128)(2,1)}, u32[]{:S(2)}) copy-start(bf16[2,128,1024]{2,1,0:T(8,128)(2,1)} %param.17) | copy-start | bytes 1572868
  11.0 118.5 %reduce-scatter.8.cloned.1.call-start = ((), (), s32[]{:S(2)}) async-start(), calls=%async_computation.4 | async-start | bytes 2293760 | tf_op jit(solution)/shard_map/reduce_scatter | solution.py:53
  98.9 700.2 %reduce-scatter.12.cloned.1.call-start = ((), (), s32[]{:S(2)}) async-start(), calls=%async_computation.7 | async-start | bytes 1146880
  130.9 637.3 %copy-start.9 = (bf16[2,32,16]{1,2,0:T(8,128)(2,1)S(1)}, bf16[2,32,16]{1,2,0:T(8,128)(2,1)}, u32[]{:S(2)}) copy-start(bf16[2,32,16]{1,2,0:T(8,128)(2,1)} %copy.21) | copy-start | bytes 6148
  768.3 1.7 copy-start.1
  769.9 525.3 %all-gather.6.cloned.1.call-start = ((), (), s32[]{:S(2)}) async-start(), calls=%async_computation.5 | async-start | bytes 2293760 | tf_op jit(solution)/shard_map/all_gather | solution.py:94
  1295.2 5.5 copy-start.8
Sparse Core Ops, SparseCore 0:
  11.2 81.4 all-gather.3
Sparse Core Ops, SparseCore 1:
  12.6 30.7 reduce-scatter.9
  99.0 30.5 reduce-scatter.7
  769.9 29.1 reduce-scatter.11
  802.0 36.1 all-gather.5
where the time goes:
time: 1310 us
  blocking collectives  1140 us (87%)
  waiting for transfers between devices  125 us (10%)
  matrix products  16.9 us (1%)
  between operations  15.9 us (1%)
    psum x1, blocking collectives, on_device(): lax.psum((down_local, up_share), ('dp', 'cand'))  495 us
    psum x1, blocking collectives, on_device(): summed_grad, loss_sum = lax.psum((score_vector, total), ('cand', 'tensor'))  493 us
    all_gather x1, blocking collectives, on_device(): all_scores = lax.all_gather(scores, ('cand', 'tensor'), axis=1, tiled=True)  140 us
    all_gather x1, waiting for transfers between devices, on_device(): full_weight = lax.all_gather(out_weight, 'cand', axis=0, tiled=True)  81.7 us
    reduce_scatter x1, waiting for transfers between devices, on_device(): lax.psum_scatter(head_terms.astype(jnp.bfloat16), 'tensor', scatter_dimen...  29 us
  transfers between devices with their start and end apart: 5, of which 3 were waited for; matrix products, arithmetic and copies ran while one was open for 1% of the time, Pallas kernels for 0%

commit v1 on v0

--- a/solution.py
+++ b/solution.py
@@ -111,7 +111,9 @@
     down_local = jnp.einsum(
         "qch,qcr->hr", context, full_adapter, preferred_element_type=jnp.float32
     )
-    down_grad, up_weight_gradient = lax.psum((down_local, up_share), ("dp", "cand"))
+    down_grad, up_weight_gradient = lax.psum(
+        lax.psum((down_local, up_share), axis_name="cand"), axis_name="dp"
+    )
     return (context_grad, grad_rows, down_grad, up_weight_gradient, pair_loss)
 
 

time: 1310 us -> 959 us (0.73)
  the two profiles are of different devices: /device:TPU:16 before, /device:TPU:8 now
where the time goes in v1:
time: 959 us
  blocking collectives  739 us (77%)
  waiting for transfers between devices  175 us (18%)
  matrix products  16.9 us (2%)
  between operations  16 us (2%)
    psum x1, blocking collectives, on_device(): summed_grad, loss_sum = lax.psum((score_vector, total), ('cand', 'tensor'))  492 us
    all_gather x1, blocking collectives, on_device(): all_scores = lax.all_gather(scores, ('cand', 'tensor'), axis=1, tiled=True)  141 us
    psum x1, blocking collectives, on_device(): lax.psum((down_local, up_share), axis_name='cand')  93.2 us
    all_gather x1, waiting for transfers between devices, on_device(): full_weight = lax.all_gather(out_weight, 'cand', axis=0, tiled=True)  81.7 us
    psum x1, waiting for transfers between devices, on_device(): lax.psum(lax.psum((down_local, up_share), axis_name='cand'), axis_name='dp')  48.9 us
    reduce_scatter x1, waiting for transfers between devices, on_device(): lax.psum_scatter(head_terms.astype(jnp.bfloat16), 'tensor', scatter_dimen...  29.4 us
  transfers between devices with their start and end apart: 6, of which 4 were waited for; matrix products, arithmetic and copies ran while one was open for 2% of the time, Pallas kernels for 0%

profile of v1, /device:TPU:8, one launch (start us, length us, event | category | flops | bytes accessed | tf_op | source)
XLA Modules:
  0.0 958.7 jit_solution(11741534377837041497)
XLA Ops:
  8.1 0.7 all-gather.4.cloned.1.call-update
  8.8 0.2 copy-done
  9.0 0.9 convolution_convert_fusion
  10.0 0.2 copy.20
  10.2 0.7 reshape.41
  11.0 81.7 %all-gather.4.cloned.1.call-done = bf16[3584,896]{1,0:T(8,128)(2,1)} async-done(((bf16[112,896]{1,0:T(8,128)(2,1)}), bf16[3584,896]{1,0:T(8,128)(2,1)}) %all-gather.4.cloned.1.call-update) | async-done | bytes 6422544 | tf_op jit(solution)/shard_map/all_gather | solution.py:49
  92.7 6.2 fusion.4
  99.0 0.8 reshape.42
  99.8 0.7 copy.21
  100.4 29.4 %reduce-scatter.8.cloned.1.call-done = bf16[2,32,3584]{2,1,0:T(8,128)(2,1)} async-done(((bf16[2,128,3584]{2,1,0:T(8,128)(2,1)}), bf16[2,32,3584]{2,1,0:T(8,128)(2,1)}) %reduce-scatter.8.cloned.1.call-update) | async-done | bytes 458768 | tf_op jit(solution)/shard_map/reduce_scatter | solution.py:53
  129.9 1.4 multiply_reduce_fusion.2
  131.4 0.3 multiply_reduce_fusion.1
  131.6 140.7 %all-gather = f32[128,32,2]{1,2,0:T(2,128)S(1)} all-gather(f32[1,32,2]{1,2,0:T(2,128)S(1)} %bitcast.57), channel_id=1, replica_groups=mesh['dp'=4,'cand'=32,'tensor'=4] {'cand','tensor'}, dimensions={0}, use_global_device_ids=true | all-gather | bytes 33024 | tf_op jit(solution)/shard_map/all_gather | solution.py:70
  272.5 1.2 fusion.24
  274.0 491.7 %all-reduce = (f32[2,4096]{1,0:T(2,128)S(1)}, f32[2]{0:T(128)S(1)}, f32[2]{0:T(128)S(1)}) all-reduce(f32[2,4096]{1,0:T(2,128)S(1)} %sub.29, f32[2]{0:T(128)S(1)} %get-tuple-element.6, f32[2]{0:T(128)S(1)} %get-tuple-element.5), channel_id=1, replica_groups=mesh['dp'=4,'cand'=32,'tensor'=4] {'cand','tensor'}, use_global_device_ids=true, to_apply=%region_6.7 | all-reduce | flops 8196 | bytes 65568 | tf_op jit(solution)/shard_map/psum | solution.py:78
  765.7 1.2 fusion.32
  767.0 0.3 multiply_reduce_fusion
  767.3 0.3 subtract_convert_fusion
  767.6 0.2 fusion.11
  767.8 1.3 copy.22
  769.2 0.7 all-gather.6.cloned.1.call-update
  769.9 1.4 fusion.13
  771.5 13.4 %all_gather.15 = bf16[2,128,16]{2,0,1:T(2,128)(2,1)S(1)} all-gather(bf16[2,32,16]{2,0,1:T(2,128)(2,1)S(1)} %copy.17), channel_id=1, replica_groups=mesh['dp'=4,'cand'=32,'tensor'=4] {'tensor'}, dimensions={1}, use_global_device_ids=true | all-gather | bytes 10240 | tf_op jit(solution)/shard_map/all_gather | solution.py:95
  784.9 0.2 convolution_bitcast_fusion.1
  785.1 13.3 %reduce-scatter.12.cloned.1.call-done = bf16[896,16]{1,0:T(8,128)(2,1)} async-done(((bf16[3584,16]{1,0:T(8,128)(2,1)}), bf16[896,16]{1,0:T(8,128)(2,1)}) %reduce-scatter.12.cloned.1.call-update) | async-done | bytes 28688
  798.4 1.0 copy.23
  799.4 93.2 %all-reduce.7 = (f32[896,16]{0,1:T(8,128)}, f32[16,896]{1,0:T(8,128)}) all-reduce(f32[896,16]{0,1:T(8,128)S(1)} %convolution_bitcast_fusion.1, bf16[16,896]{1,0:T(8,128)(2,1)S(1)} %copy.23), channel_id=1, replica_groups=mesh['dp'=4,'cand'=32,'tensor'=4] {'cand'}, use_global_device_ids=true, to_apply=%region_10.11 | all-reduce | flops 28672 | bytes 200704 | tf_op jit(solution)/shard_map/psum | solution.py:115
  892.7 5.5 fusion
  898.2 1.1 fusion.12
  899.3 48.9 %all-reduce.6.cloned.1.call-done = (f32[896,16]{0,1:T(8,128)}, f32[16,896]{1,0:T(8,128)}) async-done(((f32[896,16]{0,1:T(8,128)}, f32[16,896]{1,0:T(8,128)}), (f32[896,16]{0,1:T(8,128)}, f32[16,896]{1,0:T(8,128)})) %all-reduce.6.cloned.1.call-update) | async-done | bytes 114704 | tf_op jit(solution)/shard_map/psum | solution.py:114
  948.2 1.4 copy.31
  949.6 1.4 copy.32
  (46 shorter events, 1.1 us)
Async XLA Ops:
  8.0 1.0 copy-start
  8.0 84.7 %all-gather.4.cloned.1.call-start = ((), (), s32[]{:S(2)}) async-start(), calls=%async_computation.3 | async-start | bytes 6623232 | tf_op jit(solution)/shard_map/all_gather | solution.py:49
  8.7 90.2 %reduce-scatter.10.cloned.1.call-start = ((), (), s32[]{:S(2)}) async-start(), calls=%async_computation.6 | async-start | bytes 40960
  10.9 119.0 %copy-start.4 = (bf16[2,32,3584]{2,1,0:T(8,128)(2,1)S(1)}, bf16[2,32,3584]{2,1,0:T(8,128)(2,1)}, u32[]{:S(2)}) copy-start(bf16[2,32,3584]{2,1,0:T(8,128)(2,1)} %param.11) | copy-start | bytes 1376260
  10.9 119.0 %copy-start.5 = (bf16[16,3584]{1,0:T(8,128)(2,1)S(1)}, bf16[16,3584]{1,0:T(8,128)(2,1)}, u32[]{:S(2)}) copy-start(bf16[16,3584]{1,0:T(8,128)(2,1)} %param.14) | copy-start | bytes 344068
  10.9 120.4 %copy-start.6 = (f32[3584]{0:T(1024)S(1)}, f32[3584]{0:T(1024)}, u32[]{:S(2)}) copy-start(f32[3584]{0:T(1024)} %param.16) | copy-start | bytes 43012
  10.9 120.4 %copy-start.7 = (f32[3584]{0:T(1024)S(1)}, f32[3584]{0:T(1024)}, u32[]{:S(2)}) copy-start(f32[3584]{0:T(1024)} %param.15) | copy-start | bytes 43012
  10.9 261.6 %copy-start.2 = (s32[2,128,1024]{2,1,0:T(8,128)S(1)}, s32[2,128,1024]{2,1,0:T(8,128)}, u32[]{:S(2)}) copy-start(s32[2,128,1024]{2,1,0:T(8,128)} %param.18) | copy-start | bytes 3145732
  11.0 261.6 %copy-start.3 = (bf16[2,128,1024]{2,1,0:T(8,128)(2,1)S(1)}, bf16[2,128,1024]{2,1,0:T(8,128)(2,1)}, u32[]{:S(2)}) copy-start(bf16[2,128,1024]{2,1,0:T(8,128)(2,1)} %param.17) | copy-start | bytes 1572868
  11.0 118.9 %reduce-scatter.8.cloned.1.call-start = ((), (), s32[]{:S(2)}) async-start(), calls=%async_computation.4 | async-start | bytes 2293760 | tf_op jit(solution)/shard_map/reduce_scatter | solution.py:53
  98.9 699.5 %reduce-scatter.12.cloned.1.call-start = ((), (), s32[]{:S(2)}) async-start(), calls=%async_computation.7 | async-start | bytes 1146880
  131.3 636.3 %copy-start.9 = (bf16[2,32,16]{1,2,0:T(8,128)(2,1)S(1)}, bf16[2,32,16]{1,2,0:T(8,128)(2,1)}, u32[]{:S(2)}) copy-start(bf16[2,32,16]{1,2,0:T(8,128)(2,1)} %copy.21) | copy-start | bytes 6148
  767.6 1.7 copy-start.1
  769.2 123.6 %all-gather.6.cloned.1.call-start = ((), (), s32[]{:S(2)}) async-start(), calls=%async_computation.5 | async-start | bytes 2293760 | tf_op jit(solution)/shard_map/all_gather | solution.py:94
  769.9 178.3 %all-reduce.6.cloned.1.call-start = ((), (), s32[]{:S(2)}) async-start(), calls=%async_computation.8 | async-start | bytes 229376 | tf_op jit(solution)/shard_map/psum | solution.py:114
  892.7 5.5 copy-start.8
Sparse Core Ops, SparseCore 0:
  11.2 81.4 all-gather.3
Sparse Core Ops, SparseCore 1:
  12.6 31.1 reduce-scatter.9
  99.0 30.8 reduce-scatter.7
  769.2 29.1 reduce-scatter.11
  801.3 37.2 all-gather.5
  892.8 55.4 all-reduce.5
